TPU v7x, 256 devices: a whole 4x4x8 slice. The times are simulated.
256 devices in a mesh: req: 32 (over z, x), tp: 8 (over y, core).
Axes of the slice: x: 4, y: 4, z: 8, core: 2. Of those that a mesh axis runs over, the one named last changes fastest.
Arguments:
- hidden_in: bfloat16 [192, 64, 3072], P('req', None, 'tp'), may hold values from -3 to 3
- request_order: int32 [192], replicated, may hold values from 0 to 191, as said below
- norm_gain: bfloat16 [3072], replicated, may hold values from 0.099609375 to 1.8984375
- w_query: bfloat16 [3072, 3072], P(None, 'tp'), may hold values from -0.109375 to 0.109375
- key_weight: bfloat16 [3072, 1024], P(None, 'tp'), may hold values from -0.4375 to 0.4375
- value_weight: bfloat16 [3072, 1024], P(None, 'tp'), may hold values from -0.109375 to 0.109375
- w_out: bfloat16 [3072, 3072], P('tp'), may hold values from -0.109375 to 0.109375
- key_cache: bfloat16 [192, 8, 3456, 128], P('req', 'tp'), may hold values from -360 to 360
- cached_values: bfloat16 [192, 8, 3456, 128], P('req', 'tp'), may hold values from -24 to 24
- cache_lengths: int32 [192], P('req'), may hold values from 864 to 3456, as said below
- tree_parent: int32 [192, 64], P('req'), may hold values from 0 to 63, as said below
- kept_nodes: int32 [192, 8], P('req'), may hold values from 0 to 63
Outputs:
- layer_out: bfloat16 [192, 64, 3072], P('req', None, 'tp')
- appended: bfloat16 [192, 2, 8, 8, 128], P('req', None, None, 'tp')
Inputs may be any that keep to these rules, and one draw needn't show every extreme that they name: `request_order`: each request is held by exactly one slot. The 6 requests of one device's rows go to 6 different devices of req, and the slots of one device hold requests of 6 different devices. `cache_lengths`: some slot has exactly 3456 live positions. `tree_parent`: node 0 has parent 0; every other node's parent has a lower index.
All inputs are finite; a program needn't handle non-finite values.
Results may differ from a plain program's by a relative error of at most 0.0085.
The roundings to bfloat16 on the way count: a program that leaves them out, or rounds other values in their place, can miss the bound.
Values may be sent and summed in bfloat16 or wider, within the bound.
A program may use at most 128 MiB of HBM per device.

v0:
```python
import jax
import jax.numpy as jnp
from jax import lax
from jax.sharding import PartitionSpec as P

HEAD_WIDTH = 128
NORM_EPSILON = 1e-05


def rotary_embedding(vectors, token_positions):
    half_dim = vectors.shape[-1] // 2
    frequency = 500000.0 ** (-jnp.arange(half_dim, dtype=jnp.float32) * 2.0 / vectors.shape[-1])
    angles = token_positions[..., None] * frequency
    cosine = jnp.cos(angles)[..., None, :]
    sine = jnp.sin(angles)[..., None, :]
    first_half = vectors[..., :half_dim]
    second_half = vectors[..., half_dim:]
    return jnp.concatenate(
        [first_half * cosine - second_half * sine, second_half * cosine + first_half * sine],
        axis=-1,
    )


def body(
    hidden_in,
    request_order,
    norm_gain,
    w_query,
    key_weight,
    value_weight,
    w_out,
    key_cache,
    cached_values,
    cache_lengths,
    tree_parent,
    kept_nodes,
):
    slots_here = key_cache.shape[0]
    tree_length = hidden_in.shape[1]
    width_local = hidden_in.shape[2]
    local_groups = key_cache.shape[1]
    local_heads = w_query.shape[1] // HEAD_WIDTH
    group_width = local_heads // local_groups
    slot_ids = lax.axis_index("req") * slots_here + jnp.arange(slots_here, dtype=jnp.int32)
    own_order = request_order[slot_ids]
    piece = lax.all_gather(hidden_in, "req", axis=0, tiled=True)
    piece_ids = jnp.arange(piece.shape[0], dtype=jnp.int32)
    chooser = (own_order[:, None] == piece_ids[None, :]).astype(jnp.bfloat16)
    dealt = jnp.einsum("rm,mtd->rtd", chooser, piece, preferred_element_type=jnp.float32).astype(
        jnp.bfloat16
    )
    widened = lax.all_gather(dealt, "tp", axis=2, tiled=True).astype(jnp.float32)
    normalized_input = (
        widened
        * lax.rsqrt(jnp.mean(widened * widened, axis=-1, keepdims=True) + NORM_EPSILON)
        * norm_gain.astype(jnp.float32)
    ).astype(jnp.bfloat16)
    flat_rows = normalized_input.reshape(slots_here * tree_length, normalized_input.shape[2])
    query_rows = jnp.dot(flat_rows, w_query, preferred_element_type=jnp.float32).reshape(
        slots_here, tree_length, local_heads, HEAD_WIDTH
    )
    fresh_keys = jnp.dot(flat_rows, key_weight, preferred_element_type=jnp.float32).reshape(
        slots_here, tree_length, local_groups, HEAD_WIDTH
    )
    fresh_values = (
        jnp.dot(flat_rows, value_weight, preferred_element_type=jnp.float32)
        .astype(jnp.bfloat16)
        .reshape(slots_here, tree_length, local_groups, HEAD_WIDTH)
    )
    node_ids = jnp.arange(tree_length, dtype=jnp.int32)
    parent_link = (
        (tree_parent[:, :, None] == node_ids[None, None, :]) & (node_ids[None, :, None] > 0)
    ).astype(jnp.float32)
    ancestry = jnp.eye(tree_length, dtype=jnp.float32)[None] + parent_link
    for sweep in range(tree_length.bit_length()):
        ancestry = jnp.minimum(
            jnp.einsum("rij,rjk->rik", ancestry, ancestry, precision=lax.Precision.HIGHEST), 1.0
        )
    token_positions = cache_lengths.astype(jnp.float32)[:, None] + jnp.sum(ancestry, axis=-1) - 1.0
    rotated_query = (
        rotary_embedding(query_rows, token_positions)
        .astype(jnp.bfloat16)
        .reshape(slots_here, tree_length, local_groups, group_width, HEAD_WIDTH)
    )
    key_rot = rotary_embedding(fresh_keys, token_positions).astype(jnp.bfloat16)
    score_scale = HEAD_WIDTH ** (-0.5)
    cache_scores = (
        jnp.einsum(
            "rtgqd,rgcd->rgqtc", rotated_query, key_cache, preferred_element_type=jnp.float32
        )
        * score_scale
    )
    live_keys = jnp.arange(key_cache.shape[2], dtype=jnp.int32)[None, :] < cache_lengths[:, None]
    cache_scores = jnp.where(live_keys[:, None, None, None, :], cache_scores, -jnp.inf)
    tree_scores = (
        jnp.einsum("rtgqd,rsgd->rgqts", rotated_query, key_rot, preferred_element_type=jnp.float32)
        * score_scale
    )
    tree_scores = jnp.where(ancestry[:, None, None] > 0, tree_scores, -jnp.inf)
    row_max = jnp.maximum(jnp.max(cache_scores, axis=-1), jnp.max(tree_scores, axis=-1))
    cache_exp = jnp.exp(cache_scores - row_max[..., None])
    tree_exp = jnp.exp(tree_scores - row_max[..., None])
    row_total = jnp.sum(cache_exp, axis=-1) + jnp.sum(tree_exp, axis=-1)
    cache_weights = (cache_exp / row_total[..., None]).astype(jnp.bfloat16)
    tree_weights = (tree_exp / row_total[..., None]).astype(jnp.bfloat16)
    attended = jnp.einsum(
        "rgqtc,rgcd->rtgqd", cache_weights, cached_values, preferred_element_type=jnp.float32
    )
    attended = attended + jnp.einsum(
        "rgqts,rsgd->rtgqd", tree_weights, fresh_values, preferred_element_type=jnp.float32
    )
    attended = attended.astype(jnp.bfloat16).reshape(
        slots_here, tree_length, local_heads * HEAD_WIDTH
    )
    keep_select = (kept_nodes[:, :, None] == node_ids[None, None, :]).astype(jnp.bfloat16)
    stacked = jnp.stack([key_rot, fresh_values], axis=1)
    appended = jnp.einsum(
        "rkt,rxtgd->rxkgd", keep_select, stacked, preferred_element_type=jnp.float32
    ).astype(jnp.bfloat16)
    partials = jnp.dot(
        attended.reshape(-1, attended.shape[2]), w_out, preferred_element_type=jnp.float32
    )
    summed = lax.psum(partials, "tp")
    my_share = lax.dynamic_slice_in_dim(summed, lax.axis_index("tp") * width_local, width_local, 1)
    layer_out = (my_share.reshape(dealt.shape) + dealt.astype(jnp.float32)).astype(jnp.bfloat16)
    return (layer_out, appended)


def solution(mesh):
    placed = (
        P("req", None, "tp"),
        P(),
        P(),
        P(None, "tp"),
        P(None, "tp"),
        P(None, "tp"),
        P("tp", None),
        P("req", "tp", None, None),
        P("req", "tp", None, None),
        P("req"),
        P("req", None),
        P("req", None),
    )
    return jax.shard_map(
        body,
        mesh=mesh,
        in_specs=placed,
        out_specs=(P("req", None, "tp"), P("req", None, None, "tp", None)),
        check_vma=False,
    )
```

profile of v0, /device:TPU:2, one launch (start us, length us, event | category | flops | bytes accessed | tf_op | source)
XLA Modules:
  0.0 284.8 jit_solution(10960639715566622475)
XLA Ops:
  7.2 0.7 all-gather.3.cloned.1.call-update
  8.0 1.3 gather_fusion
  9.3 106.1 %all-gather.3.cloned.1.call-done = bf16[192,64,384]{2,1,0:T(8,128)(2,1)} async-done(((bf16[6,64,384]{2,1,0:T(8,128)(2,1)}), bf16[192,64,384]{2,1,0:T(8,128)(2,1)}) %all-gather.3.cloned.1.call-update) | async-done | bytes 9437200 | tf_op jit(solution)/shard_map/all_gather | solution.py:46
  115.4 11.9 %fusion.3 = bf16[6,64,384]{2,0,1:T(8,128)(2,1)S(1)} fusion(bf16[192,64,384]{2,1,0:T(8,128)(2,1)} %all-gather.3.cloned.1.call-done, s32[6]{0:T(128)S(1)} %gather_fusion), kind=kOutput, calls=%fused_computation.7 | convolution fusion | flops 56624256 | bytes 9732120 | tf_op jit(solution)/shard_map/rm,mtd->rtd/dot_general | solution.py:49
  127.3 0.8 copy.78
  128.3 0.5 convolution_minimum_fusion.6
  128.7 0.3 convolution_minimum_fusion.5
  129.0 0.3 convolution_minimum_fusion.4
  129.4 0.3 convolution_minimum_fusion.3
  129.7 0.3 convolution_minimum_fusion.2
  130.0 0.3 convolution_minimum_fusion.1
  130.4 0.4 fusion.63
  131.0 4.5 %copy.51 = bf16[3072,384]{0,1:T(8,128)(2,1)} copy(bf16[3072,384]{1,0:T(8,128)(2,1)} %param.15) | data formatting | bytes 4718592 | tf_op args[3]
  135.5 0.8 multiply_cosine_fusion.1
  136.4 19.0 %all-gather.5.cloned.1.call-done = bf16[6,64,3072]{2,1,0:T(8,128)(2,1)} async-done(((bf16[6,64,384]{2,1,0:T(8,128)(2,1)}), bf16[6,64,3072]{2,1,0:T(8,128)(2,1)}) %all-gather.5.cloned.1.call-update) | async-done | bytes 2359312 | tf_op jit(solution)/shard_map/all_gather | solution.py:52
  155.4 2.4 fusion.11
  157.7 2.4 fusion.13
  160.2 0.8 convolution_bitcast_fusion
  161.0 0.8 fusion.38
  161.8 1.4 fusion.14
  163.2 0.3 subtract_convert_fusion
  163.6 6.9 %fusion.2 = (f32[6,3,64]{2,1,0:T(4,128)S(1)}, f32[6,64,3,3456]{3,1,2,0:T(8,128)}) fusion(pred[6,3456]{1,0:T(8,128)(4,1)S(1)} %iota_compare_fusion.1, bf16[6,1,3456,128]{3,2,1,0:T(8,128)(2,1)S(1)} %bitcast.146, bf16[6,64,3,64]{3,1,2,0:T(8,128)(2,1)S(1)} %get-tuple-element.11, bf16[6,64,3,64]{3,1,2,0:T(8,128)(2,1)S(1)} %get-tuple-element.10), kind=kOutput, calls=%fused_computation.6 | convolution fusion | flops 1031748480 | bytes 21553920 | tf_op jit(solution)/shard_map/rtgqd,rgcd->rgqtc/dot_general | solution.py:88
  170.5 0.4 fusion.64
  171.1 9.2 %fusion.1 = f32[6,3,64]{2,1,0:T(4,128)S(1)} fusion(f32[6,64,3,3456]{3,1,2,0:T(8,128)} %get-tuple-element.19, f32[6,3,64]{2,1,0:T(4,128)S(1)} %max.9, pred[6,3456]{1,0:T(8,128)(4,1)S(1)} %iota_compare_fusion.1), kind=kLoop, calls=%fused_computation.5 | loop fusion | flops 15924096 | bytes 15955200 | tf_op jit(solution)/shard_map/reduce_sum | solution.py:103
  180.3 1.9 convolution_convert_fusion
  182.2 10.3 %fusion.17 = f32[6,128,3,64]{1,3,2,0:T(8,128)S(1)} fusion(bf16[6,1,3456,128]{3,2,1,0:T(8,128)(2,1)} %param.20, f32[6,3,64]{2,1,0:T(4,128)S(1)} %add.98, f32[6,3,64]{2,1,0:T(4,128)S(1)} %max.9, f32[6,64,3,3456]{3,1,2,0:T(8,128)} %get-tuple-element.19, pred[6,3456]{1,0:T(8,128)(4,1)S(1)} %iota_compare_fusion.1), kind=kOutput, calls=%fused_computation.25 | convolution fusion | flops 1039122432 | bytes 21853440 | tf_op jit(solution)/shard_map/rgqtc,rgcd->rtgqd/dot_general | solution.py:106
  192.5 0.3 fusion.24
  193.1 3.5 %fusion.28 = f32[384,3072]{1,0:T(8,128)} fusion(bf16[384,3072]{1,0:T(8,128)(2,1)S(1)} %copy-done, bf16[48,8,3,128]{3,2,1,0:T(4,128)(2,1)S(1)} %bitcast.149), kind=kOutput, calls=%fused_computation.48 | convolution fusion | flops 905969664 | bytes 7372800 | tf_op jit(solution)/shard_map/dot_general | solution.py:120
  196.7 0.8 fusion.25
  197.5 78.8 %all-reduce.2.cloned.1.call-done = f32[384,3072]{1,0:T(8,128)} async-done(((f32[384,3072]{1,0:T(8,128)}), f32[384,3072]{1,0:T(8,128)}) %all-reduce.2.cloned.1.call-update) | async-done | bytes 4718608 | tf_op jit(solution)/shard_map/psum | solution.py:123
  276.3 1.1 constant_dynamic-slice_fusion
  277.4 0.8 add_convert_fusion
  (40 shorter events, 1.0 us)
Async XLA Ops:
  7.2 185.9 %copy-start = (bf16[384,3072]{1,0:T(8,128)(2,1)S(1)}, bf16[384,3072]{1,0:T(8,128)(2,1)}, u32[]{:S(2)}) copy-start(bf16[384,3072]{1,0:T(8,128)(2,1)} %param.18) | copy-start | bytes 7077892
  7.2 108.2 %all-gather.3.cloned.1.call-start = ((), (), s32[]{:S(2)}) async-start(), calls=%async_computation | async-start | bytes 9732096 | tf_op jit(solution)/shard_map/all_gather | solution.py:46
  7.9 147.5 %all-gather.5.cloned.1.call-start = ((), (), s32[]{:S(2)}) async-start(), calls=%async_computation.1 | async-start | bytes 2654208 | tf_op jit(solution)/shard_map/all_gather | solution.py:52
  9.3 118.9 %copy-start.4 = (s32[6]{0:T(128)S(1)}, s32[6]{0:T(128)}, u32[]{:S(2)}) copy-start(s32[6]{0:T(128)} %param.21) | copy-start | bytes 76
  9.3 118.9 %copy-start.3 = (bf16[3072]{0:T(1024)(128)(2,1)S(1)}, bf16[3072]{0:T(1024)(128)(2,1)}, u32[]{:S(2)}) copy-start(bf16[3072]{0:T(1024)(128)(2,1)} %param.14) | copy-start | bytes 18436
  9.3 118.9 %copy-start.5 = (s32[6,64]{1,0:T(8,128)S(1)}, s32[6,64]{1,0:T(8,128)}, u32[]{:S(2)}) copy-start(s32[6,64]{1,0:T(8,128)} %param.22) | copy-start | bytes 4612
  128.1 148.2 %all-reduce.2.cloned.1.call-start = ((), (), s32[]{:S(2)}) async-start(), calls=%async_computation.2 | async-start | bytes 9437184 | tf_op jit(solution)/shard_map/psum | solution.py:123
  155.4 4.8 %copy-start.2 = (bf16[3072,128]{1,0:T(8,128)(2,1)S(1)}, bf16[3072,128]{1,0:T(8,128)(2,1)}, u32[]{:S(2)}) copy-start(bf16[3072,128]{1,0:T(8,128)(2,1)} %param.16) | copy-start | bytes 2359300
  155.4 6.4 %copy-start.1 = (bf16[3072,384]{0,1:T(8,128)(2,1)S(1)}, bf16[3072,384]{0,1:T(8,128)(2,1)}, u32[]{:S(2)}) copy-start(bf16[3072,384]{0,1:T(8,128)(2,1)} %copy.51) | copy-start | bytes 7077892
  160.2 3.4 %slice-start = ((s8[5308416]{0:T(1024)(128)(4,1)}), s8[4194304]{0:T(1024)(128)(4,1)S(1)}, s32[]{:S(2)}) async-start(s8[5308416]{0:T(1024)(128)(4,1)} %bitcast.145), calls=%async_computation.3 | async-start | bytes 8388608
  161.8 1.7 slice-start.1
  193.1 3.6 %copy-start.6 = (s32[6,8]{1,0:T(8,128)S(1)}, s32[6,8]{1,0:T(8,128)}, u32[]{:S(2)}) copy-start(s32[6,8]{1,0:T(8,128)} %param.23) | copy-start | bytes 580
Sparse Core Ops, SparseCore 0:
  10.6 104.8 all-gather.2
  128.2 27.0 all-gather.4
  196.8 79.4 all-reduce.1
where the time goes:
time: 285 us
  waiting for transfers between devices  205 us (72%)
  matrix products  40.8 us (14%)
  other arithmetic  17 us (6%)
  between operations  14.1 us (5%)
  local copies, waits for them, and re-layouts  8.1 us (3%)
    all_gather x1, waiting for transfers between devices, body(): piece = lax.all_gather(hidden_in, 'req', axis=0, tiled=True)  106 us
    psum x1, waiting for transfers between devices, body(): summed = lax.psum(partials, 'tp')  78.8 us
    all_gather x1, waiting for transfers between devices, body(): lax.all_gather(dealt, 'tp', axis=2, tiled=True).astype(jnp.float32)  19 us
    dot_general x1, matrix products, body(): jnp.einsum('rm,mtd->rtd', chooser, piece, preferred_element_type=jnp.floa...  11.9 us
    dot_general x1, matrix products, body(): jnp.einsum('rgqtc,rgcd->rtgqd', cache_weights, cached_values, preferred_e...  10.3 us
    reduce_sum x2, other arithmetic, body(): row_total = jnp.sum(cache_exp, axis=-1) + jnp.sum(tree_exp, axis=-1)  9.32 us
    dot_general x1, matrix products, body(): jnp.einsum('rtgqd,rgcd->rgqtc', rotated_query, key_cache, preferred_eleme...  6.91 us
  transfers between devices with their start and end apart: 3, of which 3 were waited for; matrix products, arithmetic and copies ran while one was open for 4% of the time, Pallas kernels for 0%

commit v1 on v0

--- a/solution.py
+++ b/solution.py
@@ -43,7 +43,9 @@
     group_width = local_heads // local_groups
     slot_ids = lax.axis_index("req") * slots_here + jnp.arange(slots_here, dtype=jnp.int32)
     own_order = request_order[slot_ids]
-    piece = lax.all_gather(hidden_in, "req", axis=0, tiled=True)
+    piece = jnp.concatenate(
+        lax.all_to_all(jnp.stack([hidden_in] * lax.axis_size("req")), "req", 0, 0), axis=0
+    )
     piece_ids = jnp.arange(piece.shape[0], dtype=jnp.int32)
     chooser = (own_order[:, None] == piece_ids[None, :]).astype(jnp.bfloat16)
     dealt = jnp.einsum("rm,mtd->rtd", chooser, piece, preferred_element_type=jnp.float32).astype(

time: 285 us -> 418 us (1.47)
  waiting for transfers between devices: 205 us -> 321 us
  starting transfers between devices: 0.12 us -> 12.1 us
  local copies, waits for them, and re-layouts: 8.1 us -> 13.7 us
    all_to_all x0 -> x1, waiting for transfers between devices: none -> 212 us  [body(): lax.all_to_all(jnp.stack([hidden_in] * lax.axis_size('req')), 'req', 0, 0)]
    all_gather x1 -> x0, waiting for transfers between devices: 106 us -> none  [body(): piece = lax.all_gather(hidden_in, 'req', axis=0, tiled=True)]
    all_to_all x0 -> x1, starting transfers between devices: none -> 11.8 us  [body(): lax.all_to_all(jnp.stack([hidden_in] * lax.axis_size('req')), 'req', 0, 0)]
    all_gather x1, waiting for transfers between devices: 19 us -> 30.1 us  [body(): lax.all_gather(dealt, 'tp', axis=2, tiled=True).astype(jnp.float32)]
    another operation x0 -> x1, local copies, waits for them, and re-layouts: none -> 6.35 us  [body(): jnp.stack([hidden_in] * lax.axis_size('req'))]
  transfers between devices with their start and end apart: 3 -> 3, of which waited for: 3 -> 3; matrix products, arithmetic and copies ran while one was open for 4% -> 2% of each run, Pallas kernels for 0% -> 0%
where the time goes in v1:
time: 418 us
  waiting for transfers between devices  321 us (77%)
  matrix products  39.6 us (9%)
  other arithmetic  17.1 us (4%)
  between operations  14.4 us (3%)
  local copies, waits for them, and re-layouts  13.7 us (3%)
  starting transfers between devices  12.1 us (3%)
    all_to_all x1, waiting for transfers between devices, body(): lax.all_to_all(jnp.stack([hidden_in] * lax.axis_size('req')), 'req', 0, 0)  212 us
    psum x1, waiting for transfers between devices, body(): summed = lax.psum(partials, 'tp')  78.8 us
    all_gather x1, waiting for transfers between devices, body(): lax.all_gather(dealt, 'tp', axis=2, tiled=True).astype(jnp.float32)  30.1 us
    dot_general x1, matrix products, body(): jnp.einsum('rm,mtd->rtd', chooser, piece, preferred_element_type=jnp.floa...  11.9 us
    all_to_all x1, starting transfers between devices, body(): lax.all_to_all(jnp.stack([hidden_in] * lax.axis_size('req')), 'req', 0, 0)  11.8 us
    dot_general x1, matrix products, body(): jnp.einsum('rgqtc,rgcd->rtgqd', cache_weights, cached_values, preferred_e...  10.2 us
    reduce_sum x2, other arithmetic, body(): row_total = jnp.sum(cache_exp, axis=-1) + jnp.sum(tree_exp, axis=-1)  9.32 us
  transfers between devices with their start and end apart: 3, of which 3 were waited for; matrix products, arithmetic and copies ran while one was open for 2% of the time, Pallas kernels for 0%

profile of v1, /device:TPU:2, one launch (start us, length us, event | category | flops | bytes accessed | tf_op | source)
XLA Modules:
  0.0 417.6 jit_solution(8316106347315133236)
XLA Ops:
  7.2 6.4 %stack.4 = bf16[32,6,64,384]{3,2,1,0:T(8,128)(2,1)} broadcast(bf16[6,64,384]{2,1,0:T(8,128)(2,1)} %param.12), dimensions={1,2,3} | broadcast | bytes 9732096 | tf_op jit(solution)/shard_map/stack | solution.py:47
  13.5 11.8 %all-to-all-start = ((bf16[32,6,64,384]{3,2,1,0:T(8,128)(2,1)}), bf16[32,6,64,384]{3,2,1,0:T(8,128)(2,1)}, u32[]{:S(2)}, u32[]{:S(2)}) async-start(bf16[32,6,64,384]{3,2,1,0:T(8,128)(2,1)} %stack.4), calls=%async_computation | async-start | bytes 18874368 | tf_op jit(solution)/shard_map/all_to_all | solution.py:47
  25.4 0.6 gather_fusion
  26.1 211.8 %all-to-all-done = bf16[32,6,64,384]{3,2,1,0:T(8,128)(2,1)} async-done(((bf16[32,6,64,384]{3,2,1,0:T(8,128)(2,1)}), bf16[32,6,64,384]{3,2,1,0:T(8,128)(2,1)}, u32[]{:S(2)}, u32[]{:S(2)}) %all-to-all-start) | async-done | bytes 9437216 | tf_op jit(solution)/shard_map/all_to_all | solution.py:47
  237.9 11.9 %fusion.3 = bf16[6,64,384]{2,0,1:T(8,128)(2,1)S(1)} fusion(bf16[192,64,384]{2,1,0:T(8,128)(2,1)} %bitcast.2, s32[6]{0:T(128)S(1)} %gather_fusion), kind=kOutput, calls=%fused_computation.7 | convolution fusion | flops 56624256 | bytes 9732120 | tf_op jit(solution)/shard_map/rm,mtd->rtd/dot_general | solution.py:51
  249.8 0.8 copy.64
  250.9 4.3 %copy.37 = bf16[3072,384]{0,1:T(8,128)(2,1)} copy(bf16[3072,384]{1,0:T(8,128)(2,1)} %param.15) | data formatting | bytes 4718592 | tf_op args[3]
  255.2 0.5 convolution_minimum_fusion.6
  255.6 0.3 convolution_minimum_fusion.5
  256.0 0.3 convolution_minimum_fusion.4
  256.3 0.3 convolution_minimum_fusion.3
  256.6 0.3 convolution_minimum_fusion.2
  256.9 0.3 convolution_minimum_fusion.1
  257.3 0.4 fusion.63
  258.0 0.8 multiply_cosine_fusion.1
  258.8 30.1 %all-gather.2.cloned.1.call-done = bf16[6,64,3072]{2,1,0:T(8,128)(2,1)} async-done(((bf16[6,64,384]{2,1,0:T(8,128)(2,1)}), bf16[6,64,3072]{2,1,0:T(8,128)(2,1)}) %all-gather.2.cloned.1.call-update) | async-done | bytes 2359312 | tf_op jit(solution)/shard_map/all_gather | solution.py:54
  289.0 2.4 fusion.11
  291.3 2.5 fusion.13
  293.9 1.4 fusion.14
  295.3 0.8 convolution_bitcast_fusion
  296.1 0.8 fusion.38
  297.3 6.9 %fusion.2 = (f32[6,3,64]{2,1,0:T(4,128)S(1)}, f32[6,64,3,3456]{3,1,2,0:T(8,128)}) fusion(pred[6,3456]{1,0:T(8,128)(4,1)S(1)} %iota_compare_fusion.1, bf16[6,1,3456,128]{3,2,1,0:T(8,128)(2,1)S(1)} %bitcast.147, bf16[6,64,3,64]{3,1,2,0:T(8,128)(2,1)S(1)} %get-tuple-element.9, bf16[6,64,3,64]{3,1,2,0:T(8,128)(2,1)S(1)} %get-tuple-element.8), kind=kOutput, calls=%fused_computation.6 | convolution fusion | flops 1031748480 | bytes 21553920 | tf_op jit(solution)/shard_map/rtgqd,rgcd->rgqtc/dot_general | solution.py:90
  304.1 0.4 fusion.64
  304.7 9.2 %fusion.1 = f32[6,3,64]{2,1,0:T(4,128)S(1)} fusion(f32[6,64,3,3456]{3,1,2,0:T(8,128)} %get-tuple-element.17, f32[6,3,64]{2,1,0:T(4,128)S(1)} %max.9, pred[6,3456]{1,0:T(8,128)(4,1)S(1)} %iota_compare_fusion.1), kind=kLoop, calls=%fused_computation.5 | loop fusion | flops 15924096 | bytes 15955200 | tf_op jit(solution)/shard_map/reduce_sum | solution.py:105
  314.0 10.2 %fusion.17 = f32[6,128,3,64]{1,3,2,0:T(8,128)S(1)} fusion(bf16[6,1,3456,128]{3,2,1,0:T(8,128)(2,1)} %param.20, f32[6,3,64]{2,1,0:T(4,128)S(1)} %add.98, f32[6,3,64]{2,1,0:T(4,128)S(1)} %max.9, f32[6,64,3,3456]{3,1,2,0:T(8,128)} %get-tuple-element.17, pred[6,3456]{1,0:T(8,128)(4,1)S(1)} %iota_compare_fusion.1), kind=kOutput, calls=%fused_computation.25 | convolution fusion | flops 1039122432 | bytes 21853440 | tf_op jit(solution)/shard_map/rgqtc,rgcd->rtgqd/dot_general | solution.py:108
  324.1 0.8 convolution_convert_fusion
  324.9 0.3 fusion.24
  325.6 3.6 fusion.28
  329.2 0.8 fusion.25
  330.1 78.8 %all-reduce.2.cloned.1.call-done = f32[384,3072]{1,0:T(8,128)} async-done(((f32[384,3072]{1,0:T(8,128)}), f32[384,3072]{1,0:T(8,128)}) %all-reduce.2.cloned.1.call-update) | async-done | bytes 4718608 | tf_op jit(solution)/shard_map/psum | solution.py:125
  408.8 1.1 constant_dynamic-slice_fusion
  409.9 0.8 add_convert_fusion
  (52 shorter events, 1.5 us)
Async XLA Ops:
  7.2 318.4 %copy-start = (bf16[384,3072]{1,0:T(8,128)(2,1)S(1)}, bf16[384,3072]{1,0:T(8,128)(2,1)}, u32[]{:S(2)}) copy-start(bf16[384,3072]{1,0:T(8,128)(2,1)} %param.18) | copy-start | bytes 7077892
  13.5 11.9 %copy-start.1 = (s32[192]{0:T(256)S(1)}, s32[192]{0:T(256)}, u32[]{:S(2)}) copy-start(s32[192]{0:T(256)} %param.13) | copy-start | bytes 2308
  13.5 224.3 %all-to-all-start = ((bf16[32,6,64,384]{3,2,1,0:T(8,128)(2,1)}), bf16[32,6,64,384]{3,2,1,0:T(8,128)(2,1)}, u32[]{:S(2)}, u32[]{:S(2)}) async-start(bf16[32,6,64,384]{3,2,1,0:T(8,128)(2,1)} %stack.4), calls=%async_computation | async-start | bytes 18874368 | tf_op jit(solution)/shard_map/all_to_all | solution.py:47
  25.3 263.6 %all-gather.2.cloned.1.call-start = ((), (), s32[]{:S(2)}) async-start(), calls=%async_computation.1 | async-start | bytes 2654208 | tf_op jit(solution)/shard_map/all_gather | solution.py:54
  237.9 13.0 %copy-start.6 = (bf16[3072]{0:T(1024)(128)(2,1)S(1)}, bf16[3072]{0:T(1024)(128)(2,1)}, u32[]{:S(2)}) copy-start(bf16[3072]{0:T(1024)(128)(2,1)} %param.14) | copy-start | bytes 18436
  249.8 5.3 %copy-start.7 = (s32[6]{0:T(128)S(1)}, s32[6]{0:T(128)}, u32[]{:S(2)}) copy-start(s32[6]{0:T(128)} %param.21) | copy-start | bytes 76
  249.8 5.3 %copy-start.9 = (s32[6,64]{1,0:T(8,128)S(1)}, s32[6,64]{1,0:T(8,128)}, u32[]{:S(2)}) copy-start(s32[6,64]{1,0:T(8,128)} %param.22) | copy-start | bytes 4612
  250.6 158.2 %all-reduce.2.cloned.1.call-start = ((), (), s32[]{:S(2)}) async-start(), calls=%async_computation.2 | async-start | bytes 9437184 | tf_op jit(solution)/shard_map/psum | solution.py:125
  289.0 4.9 %copy-start.2 = (bf16[3072,384]{0,1:T(8,128)(2,1)S(1)}, bf16[3072,384]{0,1:T(8,128)(2,1)}, u32[]{:S(2)}) copy-start(bf16[3072,384]{0,1:T(8,128)(2,1)} %copy.37) | copy-start | bytes 7077892
  291.3 4.0 copy-start.3
  293.8 3.4 slice-start
  293.9 3.4 slice-start.1
  296.9 7.2 %copy-start.4 = (bf16[6,64,1,64]{3,1,0,2:T(8,128)(2,1)}, bf16[6,64,1,64]{3,1,0,2:T(8,128)(2,1)S(1)}, u32[]{:S(2)}) copy-start(bf16[6,64,1,64]{3,1,0,2:T(8,128)(2,1)S(1)} %get-tuple-element.11) | copy-start | bytes 147460
  313.9 10.2 %copy-start.8 = (bf16[3072,128]{1,0:T(8,128)(2,1)S(1)}, bf16[3072,128]{1,0:T(8,128)(2,1)}, u32[]{:S(2)}) copy-start(bf16[3072,128]{1,0:T(8,128)(2,1)} %param.17) | copy-start | bytes 2359300
  324.9 0.6 copy-start.11
  325.6 3.6 copy-start.5
  325.6 3.6 copy-start.10
  325.6 3.6 copy-start.12
Sparse Core Ops, SparseCore 0:
  250.7 38.1 all-gather.1
  329.3 79.4 all-reduce.1
